TPU v7x, 32 devices: a whole 2x2x4 slice. The times are simulated.
32 devices in a mesh: blk: 16 (over z, y, x), col: 2 (over core).
Axes of the slice: x: 2, y: 2, z: 4, core: 2. Of those that a mesh axis runs over, the one named last changes fastest.
Arguments:
- queries: bfloat16 [128, 16384], P('blk', 'col'), may hold values from -6 to 6
- factor: bfloat16 [16384, 1024], P('col', 'blk'), may hold values from -0.046875 to 0.046875
- eigenvalues: float32 [1024], replicated, may hold values from 0.05 to 20
- damping: float32 [1], replicated, may hold values from 0.5 to 2
- train_rows: bfloat16 [16384, 16384], P('blk', 'col'), may hold values from -0.046875 to 0.046875
Outputs:
- scores: bfloat16 [128, 16384], P('col', 'blk')
All inputs are finite; a program needn't handle non-finite values.
Results may differ from a plain program's by a relative error of at most 0.0049.
Values may be sent and summed in bfloat16 or wider, within the bound.
A program may use at most 64 MiB of HBM per device.

v0:
```python
import functools

import jax
import jax.numpy as jnp
from jax import lax
from jax.experimental import pallas as pl
from jax.experimental.pallas import tpu as pltpu
from jax.sharding import PartitionSpec as P

MESH = pl.DeviceIdType.MESH
CONTRACT_LAST = (((1,), (1,)), ((), ()))


def fused_kernel(
    nb, queries, factor_t, eigenvalues, damping, train_rows, out,
    query_in, factor_in, train_in, part, pair_in, part_sum, part_in, scaled_out, scaled_in,
    cross_out, cross_in, pre, total, total_in,
    train_sem, own_sem, query_send, query_recv, factor_send, factor_recv,
    part_send, part_recv, scaled_send, scaled_recv, line_send, line_recv,
    side_send, side_recv, corner_send, corner_recv, pair_send, pair_recv, cross_send, cross_recv,
):
    me = lax.axis_index("blk")
    side = lax.axis_index("col")
    rows, wide = query_in.shape[1], query_in.shape[2]
    width = wide // 2
    rank = eigenvalues.shape[1]
    every = nb * rows
    half = every // 2
    members = nb // 2
    group, mine = lax.div(me, members), lax.rem(me, members)
    half_rank = rank // 4
    line = nb // 4
    px, py, pz = lax.rem(me, 2), lax.rem(lax.div(me, 2), 2), lax.div(me, 4)
    next_x = me + 1 - 2 * px
    next_y = me + 2 - 4 * py

    def span(index, size):
        return pl.ds(pl.multiple_of(index * size, size), size)

    def to_peer(source, target, send_sem, recv_sem, peer):
        return pltpu.make_async_remote_copy(
            src_ref=source, dst_ref=target, send_sem=send_sem, recv_sem=recv_sem,
            device_id={"blk": peer}, device_id_type=MESH,
        )

    def to_pair(source, target, index):
        return pltpu.make_async_remote_copy(
            src_ref=source, dst_ref=target,
            send_sem=pair_send.at[index], recv_sem=pair_recv.at[index],
            device_id={"col": 1 - side}, device_id_type=MESH,
        )

    def each_peer(body):
        def step(k, carry):
            body(lax.rem(me + k, nb))
            return carry
        lax.fori_loop(1, nb, step, 0)

    def each_member(body):
        def step(k, carry):
            body(mine + (k % 2) * (1 - 2 * lax.rem(mine, 2)) + 2 * (lax.rem(lax.div(k, 2), 2)) * (1 - 2 * lax.rem(lax.div(mine, 2), 2)) + 4 * lax.div(k, 4) * (1 - 2 * lax.div(mine, 4)))
            return carry
        lax.fori_loop(1, members, step, 0)

    def query_copy(source, peer):
        return to_peer(queries.at[:, span(lax.rem(peer, members), wide)], query_in.at[source],
                       query_send.at[peer], query_recv.at[source], peer)

    def factor_copy(source, member):
        return to_peer(factor_t.at[:, span(member, wide)], factor_in.at[source],
                       factor_send.at[member], factor_recv.at[source], group * members + member)

    def part_copy(source, member):
        return to_peer(part_sum.at[member], part_in.at[source],
                       part_send.at[member], part_recv.at[source], group * members + member)

    def scaled_copy(source, member):
        return to_peer(scaled_out, scaled_in.at[side, source],
                       scaled_send.at[member], scaled_recv.at[source], group * members + member)

    def cross_copy(k):
        return to_peer(cross_out.at[k], cross_in.at[k], cross_send.at[k], cross_recv.at[k],
                       (1 - group) * members + mine)

    def block(z, flip_x, flip_y):
        x = 1 - px if flip_x else px
        y = 1 - py if flip_y else py
        return z * 4 + y * 2 + x

    def line_copy(z, k, up):
        half_block = pre.at[block(z, False, False), pl.ds(k * half, half)]
        return to_peer(half_block, half_block, line_send.at[up, 2 * z + k],
                       line_recv.at[2 * z + k], me + (4 if up else -4))

    def side_copy(z, k, along, incoming=False):
        index = block(z, incoming and along == 0, incoming and along == 1)
        half_block = pre.at[index, pl.ds(k * half, half)]
        return to_peer(half_block, half_block, side_send.at[along, 2 * z + k],
                       side_recv.at[along, 2 * z + k], next_y if along else next_x)

    def corner_copy(z, along, incoming=False):
        index = block(z, incoming or along == 1, incoming or along == 0)
        half_block = pre.at[index, pl.ds((1 - along) * half, half)]
        return to_peer(half_block, half_block, corner_send.at[along, z],
                       corner_recv.at[along, z], next_y if along else next_x)

    def train_copy(index):
        chunk = lax.rem(index, members) * 2 + lax.div(index, members)
        return pltpu.make_async_copy(
            train_rows.at[:, span(chunk, width)], train_in.at[index], train_sem.at[index])

    own_query = pltpu.make_async_copy(
        queries.at[:, span(mine, wide)], query_in.at[me], own_sem.at[0])
    own_factor = pltpu.make_async_copy(
        factor_t.at[:, span(mine, wide)], factor_in.at[mine], own_sem.at[1])

    barrier = pltpu.get_barrier_semaphore()
    each_peer(lambda peer: pl.semaphore_signal(
        barrier, inc=1, device_id={"blk": peer}, device_id_type=MESH))
    pl.semaphore_signal(barrier, inc=1, device_id={"col": 1 - side}, device_id_type=MESH)
    pl.semaphore_wait(barrier, nb)

    own_query.start()
    own_factor.start()
    each_peer(lambda peer: query_copy(me, peer).start())
    each_member(lambda peer: factor_copy(mine, peer).start())

    def start_train(k, carry):
        train_copy(lax.rem(me + nb - k, nb)).start()
        return carry
    lax.fori_loop(0, nb, start_train, 0)

    own_query.wait()
    own_factor.wait()
    each_peer(lambda peer: query_copy(peer, peer).wait_recv())
    each_member(lambda peer: factor_copy(peer, peer).wait_recv())

    query_wide = query_in[...].astype(jnp.float32).reshape(every, wide)
    partial_value = lax.dot_general(
        query_wide.astype(jnp.bfloat16), factor_in[...].reshape(2 * half_rank, wide),
        CONTRACT_LAST, preferred_element_type=jnp.float32)
    for k in range(2):
        part[k] = partial_value[:, k * half_rank:(k + 1) * half_rank].reshape(
            members, 2 * rows, half_rank)

    exchange = to_pair(part.at[1 - side], pair_in, 0)
    exchange.start()
    own_rank = span(2 * group + side, half_rank)
    own_values = eigenvalues[:, own_rank]
    weights = own_values / (own_values + damping[0])
    exchange.wait()
    part_sum[...] = part[side] + pair_in[...]
    each_member(lambda peer: part_copy(mine, peer).start())
    part_in[mine] = part_sum[mine]
    each_member(lambda peer: part_copy(peer, peer).wait_recv())
    scaled_out[...] = jnp.sum(part_in[...], axis=0) * weights
    each_member(lambda peer: scaled_copy(mine, peer).start())
    scaled_in[side, mine] = scaled_out[...]
    each_member(lambda peer: scaled_copy(peer, peer).wait_recv())
    swap = to_pair(scaled_in.at[side], scaled_in.at[side], 2)
    swap.start()

    def correction_of(which, where):
        scaled = scaled_in[which].reshape(every, half_rank)
        first = scaled.astype(jnp.bfloat16)
        rest = scaled - first.astype(jnp.float32)
        second = rest.astype(jnp.bfloat16)
        third = (rest - second.astype(jnp.float32)).astype(jnp.bfloat16)
        slots = members // 2
        factor_half = factor_in[pl.ds(which * slots, slots), :, span(where, width)].reshape(
            half_rank, width)
        return (
            jnp.dot(third, factor_half, preferred_element_type=jnp.float32)
            + jnp.dot(second, factor_half, preferred_element_type=jnp.float32)
        ) + jnp.dot(first, factor_half, preferred_element_type=jnp.float32)

    outgoing = correction_of(side, 1 - group)
    swap.wait()
    outgoing = outgoing + correction_of(1 - side, 1 - group)
    cross_out[...] = outgoing.reshape(2, half, width)
    for k in range(2):
        cross_copy(k).start()
    correction = correction_of(side, group) + correction_of(1 - side, group)
    query_own = query_in[:, :, span(group, width)].astype(jnp.float32).reshape(every, width)

    def finish_own(k):
        cross_copy(k).wait_recv()
        rows_of = slice(k * half, (k + 1) * half)
        whole = correction[rows_of] + cross_in[k]
        pre[me, rows_of] = ((query_own[rows_of] - whole) / damping[0]).astype(jnp.bfloat16)

    def scores_of(index):
        train_copy(index).wait()
        return lax.dot_general(
            pre[index], train_in[index], CONTRACT_LAST, preferred_element_type=jnp.float32)

    def height(i):
        mirror = lax.div(pz, line // 2)
        near = pz + mirror * (line - 1 - 2 * pz)
        v = near + i * (1 - 2 * near) if i < 2 else i
        return v + mirror * (line - 1 - 2 * v)

    def pass_on(z, k):
        @pl.when((z <= pz) & (pz < line - 1))
        def _():
            line_copy(z, k, 1).start()

        @pl.when((z >= pz) & (pz > 0))
        def _():
            line_copy(z, k, 0).start()

    total[...] = jnp.zeros_like(total)
    side_lag, corner_lag = 3, 6

    def add_scores(z, flip_x, flip_y):
        total[...] += scores_of(block(z, flip_x, flip_y))

    for e in range(2 * line + corner_lag):
        if e < 2 * line:
            i, k = divmod(e, 2)
            z = height(i)
            if i > 0:
                line_copy(z, k, 1).wait_recv()
            else:
                finish_own(k)
            pass_on(z, k)
            side_copy(z, k, 0).start()
            side_copy(z, k, 1).start()
        if 0 <= e - side_lag < 2 * line:
            i, k = divmod(e - side_lag, 2)
            z = height(i)
            side_copy(z, k, k, True).wait_recv()
            corner_copy(z, 1 - k).start()
            if k == 1:
                side_copy(z, 1, 0, True).wait_recv()
                add_scores(z, True, False)
                side_copy(z, 0, 1, True).wait_recv()
                add_scores(z, False, True)
        if e < 2 * line and e % 2 == 1:
            add_scores(height(e // 2), False, False)
        if e >= corner_lag:
            i, k = divmod(e - corner_lag, 2)
            z = height(i)
            corner_copy(z, 1 - k, True).wait_recv()
            if k == 1:
                add_scores(z, True, True)

    other_rows = pl.ds(pl.multiple_of((1 - side) * half, half), half)
    own_rows = pl.ds(pl.multiple_of(side * half, half), half)
    last = to_pair(total.at[other_rows], total_in, 1)
    last.start()

    each_peer(lambda peer: query_copy(me, peer).wait_send())

    def finish(peer):
        factor_copy(mine, peer).wait_send()
        part_copy(mine, peer).wait_send()
        scaled_copy(mine, peer).wait_send()
    each_member(finish)
    for k in range(2):
        cross_copy(k).wait_send()
    for i in range(line):
        z = height(i)
        for k in range(2):
            @pl.when((z <= pz) & (pz < line - 1))
            def _():
                line_copy(z, k, 1).wait_send()

            @pl.when((z >= pz) & (pz > 0))
            def _():
                line_copy(z, k, 0).wait_send()

            for along in range(2):
                side_copy(z, k, along).wait_send()
        for along in range(2):
            corner_copy(z, along).wait_send()
    last.wait()
    out[...] = (total[own_rows, :] + total_in[...]).astype(out.dtype)


def fused(nb, queries, factor, eigenvalues, damping, train_rows):
    rows, depth = queries.shape
    rank_slice = factor.shape[1]
    width = depth // nb
    rank = eigenvalues.shape[0]
    every = nb * rows
    train = train_rows.shape[0]
    line = nb // 4
    members = nb // 2
    anywhere = pl.BlockSpec(memory_space=pl.ANY)
    vmem = pl.BlockSpec(memory_space=pltpu.VMEM)
    dma = pltpu.SemaphoreType.DMA
    f32, bf16 = jnp.float32, jnp.bfloat16
    return pl.pallas_call(
        functools.partial(fused_kernel, nb),
        out_shape=jax.ShapeDtypeStruct((every // 2, train), bf16),
        in_specs=[anywhere, anywhere, vmem, pl.BlockSpec(memory_space=pltpu.SMEM), anywhere],
        out_specs=vmem,
        scratch_shapes=[
            pltpu.VMEM((nb, rows, 2 * width), bf16),
            pltpu.VMEM((members, rank_slice, 2 * width), bf16),
            pltpu.VMEM((nb, train, width), bf16),
            pltpu.VMEM((2, members, 2 * rows, rank // 4), f32),
            pltpu.VMEM((members, 2 * rows, rank // 4), f32),
            pltpu.VMEM((members, 2 * rows, rank // 4), f32),
            pltpu.VMEM((members, 2 * rows, rank // 4), f32),
            pltpu.VMEM((2 * rows, rank // 4), f32),
            pltpu.VMEM((2, members, 2 * rows, rank // 4), f32),
            pltpu.VMEM((2, every // 2, width), f32),
            pltpu.VMEM((2, every // 2, width), f32),
            pltpu.VMEM((nb, every, width), bf16),
            pltpu.VMEM((every, train), f32),
            pltpu.VMEM((every // 2, train), f32),
            dma((nb,)), dma((2,)),
            dma((nb,)), dma((nb,)), dma((members,)), dma((members,)),
            dma((members,)), dma((members,)), dma((members,)), dma((members,)),
            dma((2, 2 * line)), dma((2 * line,)), dma((2, 2 * line)), dma((2, 2 * line)),
            dma((2, line)), dma((2, line)), dma((3,)), dma((3,)), dma((2,)), dma((2,)),
        ],
        compiler_params=pltpu.CompilerParams(
            collective_id=0, has_side_effects=True, vmem_limit_bytes=56 * 1024 * 1024),
    )(queries, factor.T, eigenvalues[None, :], damping, train_rows)


def plain(queries, factor, eigenvalues, damping, train_rows):
    damp_value = damping[0]
    weights = eigenvalues / (eigenvalues + damp_value)
    query_part = lax.all_to_all(queries, "blk", split_axis=1, concat_axis=0, tiled=True)
    factor_part = lax.all_to_all(factor, "blk", split_axis=0, concat_axis=1, tiled=True)
    partial_value = jnp.dot(query_part, factor_part, preferred_element_type=jnp.float32)
    coefficient = lax.psum(partial_value, ("blk", "col"))
    scaled = coefficient * weights[None, :]
    correction = jnp.dot(scaled, factor_part.astype(jnp.float32).T, precision=lax.Precision.HIGHEST)
    pre_part = ((query_part.astype(jnp.float32) - correction) / damp_value).astype(jnp.bfloat16)
    pre_all = lax.all_gather(pre_part, "blk", axis=1, tiled=True)
    partial_scores = jnp.einsum("qk,nk->qn", pre_all, train_rows, preferred_element_type=jnp.float32)
    scores = lax.psum_scatter(partial_scores, "col", scatter_dimension=0, tiled=True)
    return scores.astype(jnp.bfloat16)


def per_device(nb, pair, queries, factor, eigenvalues, damping, train_rows):
    rows, depth = queries.shape
    width = depth // nb
    fits = pair == 2 and width % 128 == 0 and eigenvalues.shape[0] % 512 == 0 and rows % 8 == 0 and factor.shape[1] % 16 == 0
    fits = fits and nb == 16
    if fits:
        return fused(nb, queries, factor, eigenvalues, damping, train_rows)
    return plain(queries, factor, eigenvalues, damping, train_rows)


def solution(mesh):
    in_specs = (P("blk", "col"), P("col", "blk"), P(), P(), P("blk", "col"))
    out_specs = P("col", "blk")
    body = functools.partial(per_device, mesh.shape["blk"], mesh.shape["col"])
    return jax.shard_map(
        body, mesh=mesh, in_specs=in_specs, out_specs=out_specs, check_vma=False
    )
```

profile of v0, /device:TPU:0, one launch (start us, length us, event | category | flops | bytes accessed | tf_op | source)
XLA Modules:
  0.0 75.8 jit_solution(5704314318139749437)
XLA Ops:
  0.7 73.6 %shard_map.55 = bf16[64,1024]{1,0:T(8,128)(2,1)} custom-call(bf16[8,8192]{1,0:T(8,128)(2,1)} %queries.1, bf16[64,8192]{1,0:T(8,128)(2,1)} %bitcast.2, f32[1,1024]{1,0:T(1,128)} %bitcast.3, f32[1]{0:T(128)S(6)} %copy.7.damping, bf16[1024,8192]{1,0:T(8,128)(2,1)} %train_rows.1), custom_call_target="tpu_custom_call" | custom-call | tf_op jit(solution)/shard_map/pallas_call | solution.py:294
  74.2 1.6 %copy.8 = bf16[64,1024]{1,0:T(8,128)(2,1)} copy(bf16[64,1024]{1,0:T(8,128)(2,1)} %shard_map.55) | data formatting | bytes 262144
where the time goes:
time: 76.1 us; the launch traced here: 75.8 us
  Pallas kernels  73.6 us (97%)
  local copies, waits for them, and re-layouts  1.57 us (2%)
    pallas_call x1, Pallas kernels, fused(): pl.pallas_call(functools.partial(fused_kernel, nb), out_shape=jax.ShapeDt...  73.6 us
    unnamed x1, local copies, waits for them, and re-layouts  1.57 us

commit v1 on v0

v1 whole, which is shorter than its diff:
```python
import functools

import jax
import jax.numpy as jnp
from jax import lax
from jax.experimental import pallas as pl
from jax.experimental.pallas import tpu as pltpu
from jax.sharding import PartitionSpec as P

MESH = pl.DeviceIdType.MESH
CONTRACT_LAST = (((1,), (1,)), ((), ()))


def fused_kernel(
    nb, queries, factor_t, eigenvalues, damping, train_rows, out,
    query_out, factor_out, query_in, factor_in, train_in, part, pair_in, sum_in, scaled,
    terms_out, terms_in, own_terms, pre, total, total_in,
    train_sem, load_sem, query_send, query_recv, factor_send, factor_recv,
    rows_send, rows_recv, sum_send, sum_recv, terms_send, terms_recv,
    line_send, line_recv, side_send, side_recv, corner_send, corner_recv, pair_send, pair_recv,
):
    me = lax.axis_index("blk")
    side = lax.axis_index("col")
    rows, depth = queries.shape
    plane_size = 4
    line = nb // plane_size
    wide = depth // plane_size
    width = wide // line
    piece = width // 2
    every = nb * rows
    half = every // 2
    rank_slice = factor_t.shape[0]
    plane_rank = plane_size * rank_slice
    px, py, pz = lax.rem(me, 2), lax.rem(lax.div(me, 2), 2), lax.div(me, 4)
    z_low, z_high = lax.rem(pz, 2), lax.div(pz, 2)

    def flip(bit, yes):
        return 1 - bit if yes else bit

    def spot(k):
        return flip(px, k & 1) + 2 * flip(py, k & 2)

    def height_at(d):
        return flip(z_low, d & 1) + 2 * flip(z_high, d & 2)

    def chip(d, k):
        return height_at(d) * plane_size + spot(k)

    def span(index, size):
        return pl.ds(pl.multiple_of(index * size, size), size)

    def to_chip(source, target, send_sem, recv_sem, peer):
        return pltpu.make_async_remote_copy(
            src_ref=source, dst_ref=target, send_sem=send_sem, recv_sem=recv_sem,
            device_id={"blk": peer}, device_id_type=MESH,
        )

    def to_pair(source, target, index):
        return pltpu.make_async_remote_copy(
            src_ref=source, dst_ref=target,
            send_sem=pair_send.at[index], recv_sem=pair_recv.at[index],
            device_id={"col": 1 - side}, device_id_type=MESH,
        )

    def load_query(k):
        target = query_out.at[k - 1] if k else query_in.at[me]
        return pltpu.make_async_copy(queries.at[:, span(spot(k), wide)], target, load_sem.at[0, k])

    def load_factor(k):
        target = factor_out.at[k - 1] if k else factor_in.at[spot(0)]
        return pltpu.make_async_copy(factor_t.at[:, span(spot(k), wide)], target, load_sem.at[1, k])

    def query_copy(k, source):
        return to_chip(query_out.at[k - 1], query_in.at[source],
                       query_send.at[k - 1], query_recv.at[k - 1], chip(0, k))

    def factor_copy(k, source):
        return to_chip(factor_out.at[k - 1], factor_in.at[source],
                       factor_send.at[k - 1], factor_recv.at[k - 1], chip(0, k))

    def rows_copy(d, k, source):
        return to_chip(query_in.at[source], query_in.at[source],
                       rows_send.at[d - 1, k], rows_recv.at[d - 1, k], chip(d, 0))

    def sum_copy(k):
        return to_chip(part, sum_in.at[k - 1], sum_send.at[k - 1], sum_recv.at[k - 1], chip(0, k))

    def terms_copy(d, k):
        return to_chip(terms_out.at[d - 1, k], terms_in.at[d - 1, k],
                       terms_send.at[d - 1, k], terms_recv.at[d - 1, k], chip(d, 0))

    def block(z, flip_x, flip_y):
        return z * plane_size + flip(py, flip_y) * 2 + flip(px, flip_x)

    def piece_of(index, k):
        return pre.at[index, :, pl.ds(k * piece, piece)]

    def line_copy(z, k, up):
        ref = piece_of(block(z, False, False), k)
        return to_chip(ref, ref, line_send.at[up, 2 * z + k], line_recv.at[2 * z + k],
                       me + (plane_size if up else -plane_size))

    next_x, next_y = chip(0, 1), chip(0, 2)

    def side_copy(z, k, along, incoming=False):
        ref = piece_of(block(z, incoming and along == 0, incoming and along == 1), k)
        return to_chip(ref, ref, side_send.at[along, 2 * z + k], side_recv.at[along, 2 * z + k],
                       next_y if along else next_x)

    def corner_copy(z, along, incoming=False):
        ref = piece_of(block(z, incoming or along == 1, incoming or along == 0), 1 - along)
        return to_chip(ref, ref, corner_send.at[along, z], corner_recv.at[along, z],
                       next_y if along else next_x)

    def train_copy(index):
        z, place = lax.div(index, plane_size), lax.rem(index, plane_size)
        return pltpu.make_async_copy(
            train_rows.at[:, span(place * line + z, width)], train_in.at[index], train_sem.at[index])

    for k in range(plane_size):
        load_query(k).start()
    for k in (3, 1, 2, 0):
        load_factor(k).start()

    barrier = pltpu.get_barrier_semaphore()
    for k in range(1, plane_size):
        pl.semaphore_signal(barrier, inc=1, device_id={"blk": chip(0, k)}, device_id_type=MESH)
    for d in range(1, line):
        pl.semaphore_signal(barrier, inc=1, device_id={"blk": chip(d, 0)}, device_id_type=MESH)
    pl.semaphore_signal(barrier, inc=1, device_id={"col": 1 - side}, device_id_type=MESH)
    pl.semaphore_wait(barrier, plane_size + line - 1)

    for k in (3, 1, 2):
        load_query(k).wait()
        query_copy(k, me).start()
    for k in (3, 1, 2):
        load_factor(k).wait()
        factor_copy(k, spot(0)).start()
    load_query(0).wait()
    for d in (2, 3, 1):
        rows_copy(d, 0, me).start()

    def start_train(k, carry):
        train_copy(lax.rem(me + nb - k, nb)).start()
        return carry
    lax.fori_loop(0, nb, start_train, 0)

    for k in range(1, plane_size):
        query_copy(k, chip(0, k)).wait_recv()
        for d in (2, 3, 1):
            rows_copy(d, k, chip(0, k)).start()
    load_factor(0).wait()
    for k in (1, 2, 3):
        factor_copy(k, spot(k)).wait_recv()
    for d in range(1, line):
        for k in range(plane_size):
            rows_copy(d, k, chip(d, k)).wait_recv()

    query_wide = query_in[...].astype(jnp.float32).reshape(every, wide).astype(jnp.bfloat16)
    partial_value = lax.dot_general(
        query_wide, factor_in[...].reshape(plane_rank, wide),
        CONTRACT_LAST, preferred_element_type=jnp.float32)
    part[...] = partial_value

    own_values = eigenvalues[:, span(pz, plane_rank)]
    weights = own_values / (own_values + damping[0])

    @pl.when(side == 0)
    def _():
        to_pair(part, pair_in, 0).start()
        to_pair(scaled, scaled, 1).wait_recv()
        to_pair(part, pair_in, 0).wait_send()

    @pl.when(side == 1)
    def _():
        to_pair(part, pair_in, 0).wait_recv()
        part[...] = part[...] + pair_in[...]
        for k in (3, 1, 2):
            sum_copy(k).start()
        for k in (1, 2, 3):
            sum_copy(k).wait_recv()
        whole = ((part[...] + sum_in[0]) + (sum_in[1] + sum_in[2])) * weights
        first = whole.astype(jnp.bfloat16)
        scaled[0:every] = first
        scaled[every:2 * every] = (whole - first.astype(jnp.float32)).astype(jnp.bfloat16)
        to_pair(scaled, scaled, 1).start()

    def terms_of(z):
        both = jnp.dot(scaled[...], factor_in[:, :, span(z, width)].reshape(plane_rank, width),
                       preferred_element_type=jnp.float32)
        return both[:every] + both[every:]

    for d in (3, 2, 1):
        terms = terms_of(height_at(d)).astype(jnp.bfloat16)
        for k in range(2):
            terms_out[d - 1, k] = terms[:, k * piece:(k + 1) * piece]
            terms_copy(d, k).start()
    own_terms[...] = terms_of(pz)
    inverse = 1.0 / damping[0]

    def finish_own(k):
        for d in (1, 2, 3):
            terms_copy(d, k).wait_recv()
        whole = own_terms[:, k * piece:(k + 1) * piece] + (
            (terms_in[0, k].astype(jnp.float32) + terms_in[1, k].astype(jnp.float32))
            + terms_in[2, k].astype(jnp.float32))
        start = pl.multiple_of(pz * width + k * piece, piece)
        own = query_in[:, :, pl.ds(start, piece)].astype(jnp.float32).reshape(every, piece)
        pre[me, :, k * piece:(k + 1) * piece] = ((own - whole) * inverse).astype(jnp.bfloat16)

    def scores_of(index):
        train_copy(index).wait()
        return lax.dot_general(
            pre[index], train_in[index], CONTRACT_LAST, preferred_element_type=jnp.float32)

    def height(i):
        mirror = lax.div(pz, line // 2)
        near = pz + mirror * (line - 1 - 2 * pz)
        v = near + i * (1 - 2 * near) if i < 2 else i
        return v + mirror * (line - 1 - 2 * v)

    def pass_on(z, k):
        @pl.when((z <= pz) & (pz < line - 1))
        def _():
            line_copy(z, k, 1).start()

        @pl.when((z >= pz) & (pz > 0))
        def _():
            line_copy(z, k, 0).start()

    total[...] = jnp.zeros_like(total)
    side_lag, corner_lag = 3, 6

    def add_scores(z, flip_x, flip_y):
        total[...] += scores_of(block(z, flip_x, flip_y))

    for e in range(2 * line + corner_lag):
        if e < 2 * line:
            i, k = divmod(e, 2)
            z = height(i)
            if i > 0:
                line_copy(z, k, 1).wait_recv()
            else:
                finish_own(k)
            pass_on(z, k)
            side_copy(z, k, 0).start()
            side_copy(z, k, 1).start()
        if 0 <= e - side_lag < 2 * line:
            i, k = divmod(e - side_lag, 2)
            z = height(i)
            side_copy(z, k, k, True).wait_recv()
            corner_copy(z, 1 - k).start()
            if k == 1:
                side_copy(z, 1, 0, True).wait_recv()
                add_scores(z, True, False)
                side_copy(z, 0, 1, True).wait_recv()
                add_scores(z, False, True)
        if e < 2 * line and e % 2 == 1:
            add_scores(height(e // 2), False, False)
        if e >= corner_lag:
            i, k = divmod(e - corner_lag, 2)
            z = height(i)
            corner_copy(z, 1 - k, True).wait_recv()
            if k == 1:
                add_scores(z, True, True)

    other_rows = pl.ds(pl.multiple_of((1 - side) * half, half), half)
    own_rows = pl.ds(pl.multiple_of(side * half, half), half)
    last = to_pair(total.at[other_rows], total_in, 2)
    last.start()

    for k in range(1, plane_size):
        query_copy(k, me).wait_send()
        factor_copy(k, spot(0)).wait_send()
    for d in range(1, line):
        for k in range(plane_size):
            rows_copy(d, k, chip(0, k)).wait_send()
        for k in range(2):
            terms_copy(d, k).wait_send()

    @pl.when(side == 1)
    def _():
        for k in range(1, plane_size):
            sum_copy(k).wait_send()
        to_pair(scaled, scaled, 1).wait_send()

    for i in range(line):
        z = height(i)
        for k in range(2):
            @pl.when((z <= pz) & (pz < line - 1))
            def _():
                line_copy(z, k, 1).wait_send()

            @pl.when((z >= pz) & (pz > 0))
            def _():
                line_copy(z, k, 0).wait_send()

            for along in range(2):
                side_copy(z, k, along).wait_send()
        for along in range(2):
            corner_copy(z, along).wait_send()
    last.wait()
    out[...] = (total[own_rows, :] + total_in[...]).astype(out.dtype)


def fused(nb, queries, factor, eigenvalues, damping, train_rows):
    rows, depth = queries.shape
    rank_slice = factor.shape[1]
    plane_size = 4
    line = nb // plane_size
    wide = depth // plane_size
    width = wide // line
    every = nb * rows
    train = train_rows.shape[0]
    plane_rank = plane_size * rank_slice
    anywhere = pl.BlockSpec(memory_space=pl.ANY)
    vmem = pl.BlockSpec(memory_space=pltpu.VMEM)
    dma = pltpu.SemaphoreType.DMA
    f32, bf16 = jnp.float32, jnp.bfloat16
    return pl.pallas_call(
        functools.partial(fused_kernel, nb),
        out_shape=jax.ShapeDtypeStruct((every // 2, train), bf16),
        in_specs=[anywhere, anywhere, vmem, pl.BlockSpec(memory_space=pltpu.SMEM), anywhere],
        out_specs=vmem,
        scratch_shapes=[
            pltpu.VMEM((plane_size - 1, rows, wide), bf16),
            pltpu.VMEM((plane_size - 1, rank_slice, wide), bf16),
            pltpu.VMEM((nb, rows, wide), bf16),
            pltpu.VMEM((plane_size, rank_slice, wide), bf16),
            pltpu.VMEM((nb, train, width), bf16),
            pltpu.VMEM((every, plane_rank), f32),
            pltpu.VMEM((every, plane_rank), f32),
            pltpu.VMEM((plane_size - 1, every, plane_rank), f32),
            pltpu.VMEM((2 * every, plane_rank), bf16),
            pltpu.VMEM((line - 1, 2, every, width // 2), bf16),
            pltpu.VMEM((line - 1, 2, every, width // 2), bf16),
            pltpu.VMEM((every, width), f32),
            pltpu.VMEM((nb, every, width), bf16),
            pltpu.VMEM((every, train), f32),
            pltpu.VMEM((every // 2, train), f32),
            dma((nb,)), dma((2, plane_size)),
            dma((plane_size - 1,)), dma((plane_size - 1,)),
            dma((plane_size - 1,)), dma((plane_size - 1,)),
            dma((line - 1, plane_size)), dma((line - 1, plane_size)),
            dma((plane_size - 1,)), dma((plane_size - 1,)),
            dma((line - 1, 2)), dma((line - 1, 2)),
            dma((2, 2 * line)), dma((2 * line,)), dma((2, 2 * line)), dma((2, 2 * line)),
            dma((2, line)), dma((2, line)), dma((3,)), dma((3,)),
        ],
        compiler_params=pltpu.CompilerParams(
            collective_id=0, has_side_effects=True, vmem_limit_bytes=56 * 1024 * 1024),
    )(queries, factor.T, eigenvalues[None, :], damping, train_rows)


def plain(queries, factor, eigenvalues, damping, train_rows):
    damp_value = damping[0]
    weights = eigenvalues / (eigenvalues + damp_value)
    query_part = lax.all_to_all(queries, "blk", split_axis=1, concat_axis=0, tiled=True)
    factor_part = lax.all_to_all(factor, "blk", split_axis=0, concat_axis=1, tiled=True)
    partial_value = jnp.dot(query_part, factor_part, preferred_element_type=jnp.float32)
    coefficient = lax.psum(partial_value, ("blk", "col"))
    scaled = coefficient * weights[None, :]
    correction = jnp.dot(scaled, factor_part.astype(jnp.float32).T, precision=lax.Precision.HIGHEST)
    pre_part = ((query_part.astype(jnp.float32) - correction) / damp_value).astype(jnp.bfloat16)
    pre_all = lax.all_gather(pre_part, "blk", axis=1, tiled=True)
    partial_scores = jnp.einsum("qk,nk->qn", pre_all, train_rows, preferred_element_type=jnp.float32)
    scores = lax.psum_scatter(partial_scores, "col", scatter_dimension=0, tiled=True)
    return scores.astype(jnp.bfloat16)


def per_device(nb, pair, queries, factor, eigenvalues, damping, train_rows):
    rows, depth = queries.shape
    width = depth // nb
    fits = pair == 2 and width % 256 == 0 and eigenvalues.shape[0] % 512 == 0 and rows % 8 == 0 and factor.shape[1] % 16 == 0
    fits = fits and nb == 16
    if fits:
        return fused(nb, queries, factor, eigenvalues, damping, train_rows)
    return plain(queries, factor, eigenvalues, damping, train_rows)


def solution(mesh):
    in_specs = (P("blk", "col"), P("col", "blk"), P(), P(), P("blk", "col"))
    out_specs = P("col", "blk")
    body = functools.partial(per_device, mesh.shape["blk"], mesh.shape["col"])
    return jax.shard_map(
        body, mesh=mesh, in_specs=in_specs, out_specs=out_specs, check_vma=False
    )
```

time: 76.1 us -> 65.9 us (0.87)
  Pallas kernels: 73.6 us -> 63.5 us
    pallas_call x1, Pallas kernels: 73.6 us -> 63.5 us  [fused(): pl.pallas_call(functools.partial(fused_kernel, nb), out_shape=jax.ShapeDt...]
where the time goes in v1:
time: 65.9 us; the launch traced here: 65.7 us
  Pallas kernels  63.5 us (96%)
  local copies, waits for them, and re-layouts  1.57 us (2%)
  between operations  0.66 us (1%)
    pallas_call x1, Pallas kernels, fused(): pl.pallas_call(functools.partial(fused_kernel, nb), out_shape=jax.ShapeDt...  63.5 us
    unnamed x1, local copies, waits for them, and re-layouts  1.57 us

profile of v1, /device:TPU:0, one launch (start us, length us, event | category | flops | bytes accessed | tf_op | source)
XLA Modules:
  0.0 65.7 jit_solution(9905521570139247211)
XLA Ops:
  0.7 63.5 %shard_map.55 = bf16[64,1024]{1,0:T(8,128)(2,1)} custom-call(bf16[8,8192]{1,0:T(8,128)(2,1)} %queries.1, bf16[64,8192]{1,0:T(8,128)(2,1)} %bitcast.2, f32[1,1024]{1,0:T(1,128)} %bitcast.3, f32[1]{0:T(128)S(6)} %copy.7.damping, bf16[1024,8192]{1,0:T(8,128)(2,1)} %train_rows.1), custom_call_target="tpu_custom_call" | custom-call | tf_op jit(solution)/shard_map/pallas_call | solution.py:320
  64.1 1.6 %copy.8 = bf16[64,1024]{1,0:T(8,128)(2,1)} copy(bf16[64,1024]{1,0:T(8,128)(2,1)} %shard_map.55) | data formatting | bytes 262144

commit v2 on v1

--- a/solution.py
+++ b/solution.py
@@ -13,11 +13,11 @@
 
 def fused_kernel(
     nb, queries, factor_t, eigenvalues, damping, train_rows, out,
-    query_out, factor_out, query_in, factor_in, train_in, part, pair_in, sum_in, scaled,
-    terms_out, terms_in, own_terms, pre, total, total_in,
-    train_sem, load_sem, query_send, query_recv, factor_send, factor_recv,
-    rows_send, rows_recv, sum_send, sum_recv, terms_send, terms_recv,
-    line_send, line_recv, side_send, side_recv, corner_send, corner_recv, pair_send, pair_recv,
+    query_out, factor_out, query_in, factor_in, near_factor, train_in, part, pair_in, sum_in, scaled,
+    terms, terms_out, terms_in, pre, total, total_in,
+    train_sem, load_sem, query_send, query_recv, factor_send, factor_recv, near_send, near_recv,
+    rows_send, rows_recv, sum_send, sum_recv, scaled_send, scaled_recv, terms_send, terms_recv,
+    line_send, line_recv, far_send, side_send, side_recv, corner_send, corner_recv, pair_send, pair_recv,
 ):
     me = lax.axis_index("blk")
     side = lax.axis_index("col")
@@ -85,9 +85,19 @@
     def sum_copy(k):
         return to_chip(part, sum_in.at[k - 1], sum_send.at[k - 1], sum_recv.at[k - 1], chip(0, k))
 
-    def terms_copy(d, k):
-        return to_chip(terms_out.at[d - 1, k], terms_in.at[d - 1, k],
-                       terms_send.at[d - 1, k], terms_recv.at[d - 1, k], chip(d, 0))
+    def near_copy(part_index, k):
+        columns = span(height_at(3 if part_index else 1), width)
+        return to_chip(factor_in.at[spot(k), :, columns], near_factor.at[part_index, spot(k)],
+                       near_send.at[part_index, k], near_recv.at[part_index, k], chip(1, 0))
+
+    def scaled_copy(core):
+        return pltpu.make_async_remote_copy(
+            src_ref=scaled.at[0], dst_ref=scaled.at[1],
+            send_sem=scaled_send.at[core], recv_sem=scaled_recv.at[0],
+            device_id={"blk": chip(1, 0), "col": core}, device_id_type=MESH)
+
+    def terms_copy(k):
+        return to_chip(terms_out.at[k], terms_in.at[k], terms_send.at[k], terms_recv.at[k], chip(2, 0))
 
     def block(z, flip_x, flip_y):
         return z * plane_size + flip(py, flip_y) * 2 + flip(px, flip_x)
@@ -128,7 +138,9 @@
     for d in range(1, line):
         pl.semaphore_signal(barrier, inc=1, device_id={"blk": chip(d, 0)}, device_id_type=MESH)
     pl.semaphore_signal(barrier, inc=1, device_id={"col": 1 - side}, device_id_type=MESH)
-    pl.semaphore_wait(barrier, plane_size + line - 1)
+    pl.semaphore_signal(
+        barrier, inc=1, device_id={"blk": chip(1, 0), "col": 1 - side}, device_id_type=MESH)
+    pl.semaphore_wait(barrier, plane_size + line)
 
     for k in (3, 1, 2):
         load_query(k).wait()
@@ -139,6 +151,9 @@
     load_query(0).wait()
     for d in (2, 3, 1):
         rows_copy(d, 0, me).start()
+    load_factor(0).wait()
+    for part_index in (1, 0):
+        near_copy(part_index, 0).start()
 
     def start_train(k, carry):
         train_copy(lax.rem(me + nb - k, nb)).start()
@@ -149,9 +164,10 @@
         query_copy(k, chip(0, k)).wait_recv()
         for d in (2, 3, 1):
             rows_copy(d, k, chip(0, k)).start()
-    load_factor(0).wait()
     for k in (1, 2, 3):
         factor_copy(k, spot(k)).wait_recv()
+        for part_index in (1, 0):
+            near_copy(part_index, k).start()
     for d in range(1, line):
         for k in range(plane_size):
             rows_copy(d, k, chip(d, k)).wait_recv()
@@ -168,7 +184,7 @@
     @pl.when(side == 0)
     def _():
         to_pair(part, pair_in, 0).start()
-        to_pair(scaled, scaled, 1).wait_recv()
+        to_pair(scaled.at[0], scaled.at[0], 1).wait_recv()
         to_pair(part, pair_in, 0).wait_send()
 
     @pl.when(side == 1)
@@ -181,29 +197,39 @@
             sum_copy(k).wait_recv()
         whole = ((part[...] + sum_in[0]) + (sum_in[1] + sum_in[2])) * weights
         first = whole.astype(jnp.bfloat16)
-        scaled[0:every] = first
-        scaled[every:2 * every] = (whole - first.astype(jnp.float32)).astype(jnp.bfloat16)
-        to_pair(scaled, scaled, 1).start()
-
-    def terms_of(z):
-        both = jnp.dot(scaled[...], factor_in[:, :, span(z, width)].reshape(plane_rank, width),
+        scaled[0, 0:every] = first
+        scaled[0, every:2 * every] = (whole - first.astype(jnp.float32)).astype(jnp.bfloat16)
+        scaled_copy(0).start()
+        to_pair(scaled.at[0], scaled.at[0], 1).start()
+        scaled_copy(1).start()
+
+    parts = ((1, 0), (1, 1), (0, 0), (0, 1))
+
+    def product(which, factor_part):
+        both = jnp.dot(scaled[which], factor_part.reshape(plane_rank, piece),
                        preferred_element_type=jnp.float32)
         return both[:every] + both[every:]
 
-    for d in (3, 2, 1):
-        terms = terms_of(height_at(d)).astype(jnp.bfloat16)
-        for k in range(2):
-            terms_out[d - 1, k] = terms[:, k * piece:(k + 1) * piece]
-            terms_copy(d, k).start()
-    own_terms[...] = terms_of(pz)
+    for part_index, k in parts:
+        columns = span(2 * height_at(2 * part_index) + k, piece)
+        terms[part_index, k] = product(0, factor_in[:, :, columns])
+    for part_index in (1, 0):
+        for k in range(plane_size):
+            near_copy(part_index, k).wait_recv()
+    scaled_copy(0).wait_recv()
+    for part_index, k in parts:
+        near_part = near_factor[part_index, :, :, k * piece:(k + 1) * piece]
+        whole = terms[part_index, k] + product(1, near_part)
+        if part_index:
+            terms_out[k] = whole.astype(jnp.bfloat16)
+            terms_copy(k).start()
+        else:
+            terms[part_index, k] = whole
     inverse = 1.0 / damping[0]
 
     def finish_own(k):
-        for d in (1, 2, 3):
-            terms_copy(d, k).wait_recv()
-        whole = own_terms[:, k * piece:(k + 1) * piece] + (
-            (terms_in[0, k].astype(jnp.float32) + terms_in[1, k].astype(jnp.float32))
-            + terms_in[2, k].astype(jnp.float32))
+        terms_copy(k).wait_recv()
+        whole = terms[0, k] + terms_in[k].astype(jnp.float32)
         start = pl.multiple_of(pz * width + k * piece, piece)
         own = query_in[:, :, pl.ds(start, piece)].astype(jnp.float32).reshape(every, piece)
         pre[me, :, k * piece:(k + 1) * piece] = ((own - whole) * inverse).astype(jnp.bfloat16)
@@ -229,41 +255,130 @@
             line_copy(z, k, 0).start()
 
     total[...] = jnp.zeros_like(total)
-    side_lag, corner_lag = 3, 6
-
     def add_scores(z, flip_x, flip_y):
         total[...] += scores_of(block(z, flip_x, flip_y))
 
-    for e in range(2 * line + corner_lag):
-        if e < 2 * line:
-            i, k = divmod(e, 2)
-            z = height(i)
-            if i > 0:
-                line_copy(z, k, 1).wait_recv()
-            else:
-                finish_own(k)
-            pass_on(z, k)
-            side_copy(z, k, 0).start()
-            side_copy(z, k, 1).start()
-        if 0 <= e - side_lag < 2 * line:
-            i, k = divmod(e - side_lag, 2)
-            z = height(i)
-            side_copy(z, k, k, True).wait_recv()
-            corner_copy(z, 1 - k).start()
-            if k == 1:
-                side_copy(z, 1, 0, True).wait_recv()
-                add_scores(z, True, False)
-                side_copy(z, 0, 1, True).wait_recv()
-                add_scores(z, False, True)
-        if e < 2 * line and e % 2 == 1:
-            add_scores(height(e // 2), False, False)
-        if e >= corner_lag:
-            i, k = divmod(e - corner_lag, 2)
-            z = height(i)
-            corner_copy(z, 1 - k, True).wait_recv()
-            if k == 1:
-                add_scores(z, True, True)
-
+    direct_line, direct_corner = (True, False), (((3, 1),), ())
+
+    def for_cores(chosen, body, otherwise=None):
+        if chosen[0] == chosen[1]:
+            if chosen[0]:
+                body()
+            elif otherwise:
+                otherwise()
+            return
+        pl.when(side == (1 if chosen[1] else 0))(body)
+        if otherwise:
+            pl.when(side == (0 if chosen[1] else 1))(otherwise)
+
+    def far_copy(d, k):
+        ref = piece_of(me, k)
+        return to_chip(ref, ref, far_send.at[d - 1, k], line_recv.at[2 * pz + k], chip(d, 0))
+
+    def diagonal_copy(z, k):
+        ref = piece_of(block(z, False, False), k)
+        return to_chip(ref, ref, corner_send.at[1 - k, z], corner_recv.at[1 - k, z], chip(0, 3))
+
+    def at_corner(i, k):
+        return tuple((i, k) in direct_corner[core] for core in range(2))
+
+    def start_line(i, k):
+        def direct():
+            if i == 0:
+                for d in (3, 2, 1):
+                    far_copy(d, k).start()
+        for_cores(direct_line, direct, lambda: pass_on(height(i), k))
+
+    def line_sent(i, k):
+        z = height(i)
+
+        def direct():
+            if i == 0:
+                for d in (3, 2, 1):
+                    far_copy(d, k).wait_send()
+
+        def relayed():
+            @pl.when((z <= pz) & (pz < line - 1))
+            def _():
+                line_copy(z, k, 1).wait_send()
+
+            @pl.when((z >= pz) & (pz > 0))
+            def _():
+                line_copy(z, k, 0).wait_send()
+        for_cores(direct_line, direct, relayed)
+
+    def arrive(i, k):
+        z = height(i)
+        if i > 0:
+            line_copy(z, k, 1).wait_recv()
+        else:
+            finish_own(k)
+        start_line(i, k)
+        for_cores(at_corner(i, k), lambda: diagonal_copy(z, k).start())
+        side_copy(z, k, k).start()
+
+    def spread(i, k):
+        side_copy(height(i), k, 1 - k).start()
+
+    def turn(i, k):
+        z = height(i)
+        side_copy(z, k, k, True).wait_recv()
+        for_cores(at_corner(i, k), lambda: None, lambda: corner_copy(z, 1 - k).start())
+
+    def add_own(i):
+        add_scores(height(i), False, False)
+
+    def add_side(i, along):
+        z = height(i)
+        side_copy(z, 1 - along, along, True).wait_recv()
+        add_scores(z, along == 0, along == 1)
+
+    def add_corner(i):
+        z = height(i)
+        for along in range(2):
+            corner_copy(z, along, True).wait_recv()
+        add_scores(z, True, True)
+
+    arrive(0, 0)
+    spread(0, 0)
+    arrive(0, 1)
+    spread(0, 1)
+    add_own(0)
+    arrive(1, 0)
+    spread(1, 0)
+    arrive(1, 1)
+    spread(1, 1)
+    turn(0, 0)
+    add_own(1)
+    arrive(2, 0)
+    spread(2, 0)
+    turn(0, 1)
+    add_side(0, 0)
+    add_side(0, 1)
+    arrive(2, 1)
+    spread(2, 1)
+    turn(1, 0)
+    add_own(2)
+    arrive(3, 0)
+    spread(3, 0)
+    turn(1, 1)
+    add_side(1, 0)
+    add_side(1, 1)
+    arrive(3, 1)
+    spread(3, 1)
+    turn(2, 0)
+    add_own(3)
+    add_corner(0)
+    turn(2, 1)
+    add_side(2, 0)
+    add_side(2, 1)
+    turn(3, 0)
+    add_corner(1)
+    turn(3, 1)
+    add_side(3, 0)
+    add_side(3, 1)
+    add_corner(2)
+    add_corner(3)
     other_rows = pl.ds(pl.multiple_of((1 - side) * half, half), half)
     own_rows = pl.ds(pl.multiple_of(side * half, half), half)
     last = to_pair(total.at[other_rows], total_in, 2)
@@ -275,26 +390,24 @@
     for d in range(1, line):
         for k in range(plane_size):
             rows_copy(d, k, chip(0, k)).wait_send()
-        for k in range(2):
-            terms_copy(d, k).wait_send()
+    for k in range(plane_size):
+        for part_index in range(2):
+            near_copy(part_index, k).wait_send()
+    for k in range(2):
+        terms_copy(k).wait_send()
 
     @pl.when(side == 1)
     def _():
         for k in range(1, plane_size):
             sum_copy(k).wait_send()
-        to_pair(scaled, scaled, 1).wait_send()
+        to_pair(scaled.at[0], scaled.at[0], 1).wait_send()
+        for core in range(2):
+            scaled_copy(core).wait_send()
 
     for i in range(line):
         z = height(i)
         for k in range(2):
-            @pl.when((z <= pz) & (pz < line - 1))
-            def _():
-                line_copy(z, k, 1).wait_send()
-
-            @pl.when((z >= pz) & (pz > 0))
-            def _():
-                line_copy(z, k, 0).wait_send()
-
+            line_sent(i, k)
             for along in range(2):
                 side_copy(z, k, along).wait_send()
         for along in range(2):
@@ -327,28 +440,30 @@
             pltpu.VMEM((plane_size - 1, rank_slice, wide), bf16),
             pltpu.VMEM((nb, rows, wide), bf16),
             pltpu.VMEM((plane_size, rank_slice, wide), bf16),
+            pltpu.VMEM((2, plane_size, rank_slice, width), bf16),
             pltpu.VMEM((nb, train, width), bf16),
             pltpu.VMEM((every, plane_rank), f32),
             pltpu.VMEM((every, plane_rank), f32),
             pltpu.VMEM((plane_size - 1, every, plane_rank), f32),
-            pltpu.VMEM((2 * every, plane_rank), bf16),
-            pltpu.VMEM((line - 1, 2, every, width // 2), bf16),
-            pltpu.VMEM((line - 1, 2, every, width // 2), bf16),
-            pltpu.VMEM((every, width), f32),
+            pltpu.VMEM((2, 2 * every, plane_rank), bf16),
+            pltpu.VMEM((2, 2, every, width // 2), f32),
+            pltpu.VMEM((2, every, width // 2), bf16),
+            pltpu.VMEM((2, every, width // 2), bf16),
             pltpu.VMEM((nb, every, width), bf16),
             pltpu.VMEM((every, train), f32),
             pltpu.VMEM((every // 2, train), f32),
             dma((nb,)), dma((2, plane_size)),
             dma((plane_size - 1,)), dma((plane_size - 1,)),
             dma((plane_size - 1,)), dma((plane_size - 1,)),
+            dma((2, plane_size)), dma((2, plane_size)),
             dma((line - 1, plane_size)), dma((line - 1, plane_size)),
             dma((plane_size - 1,)), dma((plane_size - 1,)),
-            dma((line - 1, 2)), dma((line - 1, 2)),
-            dma((2, 2 * line)), dma((2 * line,)), dma((2, 2 * line)), dma((2, 2 * line)),
+            dma((2,)), dma((1,)), dma((2,)), dma((2,)),
+            dma((2, 2 * line)), dma((2 * line,)), dma((line - 1, 2)), dma((2, 2 * line)), dma((2, 2 * line)),
             dma((2, line)), dma((2, line)), dma((3,)), dma((3,)),
         ],
         compiler_params=pltpu.CompilerParams(
-            collective_id=0, has_side_effects=True, vmem_limit_bytes=56 * 1024 * 1024),
+            collective_id=0, has_side_effects=True, vmem_limit_bytes=55040 * 1024),
     )(queries, factor.T, eigenvalues[None, :], damping, train_rows)
 
 

time: 65.9 us -> 63.5 us (0.964)
  Pallas kernels: 63.5 us -> 61.1 us
    pallas_call x1, Pallas kernels: 63.5 us -> 61.1 us  [fused(): pl.pallas_call(functools.partial(fused_kernel, nb), out_shape=jax.ShapeDt...]
    unnamed x1 -> x3, local copies, waits for them, and re-layouts: 1.57 us -> 1.34 us
where the time goes in v2:
time: 63.5 us; the launch traced here: 63.1 us
  Pallas kernels  61.1 us (96%)
  local copies, waits for them, and re-layouts  1.34 us (2%)
  between operations  0.67 us (1%)
    pallas_call x1, Pallas kernels, fused(): pl.pallas_call(functools.partial(fused_kernel, nb), out_shape=jax.ShapeDt...  61.1 us
    unnamed x3, local copies, waits for them, and re-layouts  1.34 us

profile of v2, /device:TPU:0, one launch (start us, length us, event | category | flops | bytes accessed | tf_op | source)
XLA Modules:
  0.0 63.1 jit_solution(3428238167341346760)
XLA Ops:
  0.7 0.0 copy-start
  0.7 0.7 %copy-done = f32[1024]{0:T(1024)S(1)} copy-done((f32[1024]{0:T(1024)S(1)}, f32[1024]{0:T(1024)}, u32[]{:S(2)}) %copy-start) | copy-done | bytes 4120
  1.3 61.1 %shard_map.55 = bf16[64,1024]{1,0:T(8,128)(2,1)S(1)} custom-call(bf16[8,8192]{1,0:T(8,128)(2,1)} %queries.1, bf16[64,8192]{1,0:T(8,128)(2,1)} %bitcast.3, f32[1,1024]{1,0:T(1,128)S(1)} %bitcast.2, f32[1]{0:T(128)S(6)} %copy.7.damping, bf16[1024,8192]{1,0:T(8,128)(2,1)} %train_rows.1), custom_call_target="tpu_custom_call" | custom-call | tf_op jit(solution)/shard_map/pallas_call | solution.py:433
  62.5 0.7 %copy.8 = bf16[64,1024]{1,0:T(8,128)(2,1)} copy(bf16[64,1024]{1,0:T(8,128)(2,1)S(1)} %shard_map.55) | data formatting | bytes 262144
Async XLA Ops:
  0.7 0.7 %copy-start = (f32[1024]{0:T(1024)S(1)}, f32[1024]{0:T(1024)}, u32[]{:S(2)}) copy-start(f32[1024]{0:T(1024)} %param.7) | copy-start | bytes 12292

commit v3 on v2

--- a/solution.py
+++ b/solution.py
@@ -13,7 +13,7 @@
 
 def fused_kernel(
     nb, queries, factor_t, eigenvalues, damping, train_rows, out,
-    query_out, factor_out, query_in, factor_in, near_factor, train_in, part, pair_in, sum_in, scaled,
+    query_out, factor_out, query_in, factor_in, near_factor, train_in, part, pair_in, sum_in, scaled, near_scaled,
     terms, terms_out, terms_in, pre, total, total_in,
     train_sem, load_sem, query_send, query_recv, factor_send, factor_recv, near_send, near_recv,
     rows_send, rows_recv, sum_send, sum_recv, scaled_send, scaled_recv, terms_send, terms_recv,
@@ -92,7 +92,7 @@
 
     def scaled_copy(core):
         return pltpu.make_async_remote_copy(
-            src_ref=scaled.at[0], dst_ref=scaled.at[1],
+            src_ref=scaled.at[0:every], dst_ref=near_scaled,
             send_sem=scaled_send.at[core], recv_sem=scaled_recv.at[0],
             device_id={"blk": chip(1, 0), "col": core}, device_id_type=MESH)
 
@@ -184,7 +184,7 @@
     @pl.when(side == 0)
     def _():
         to_pair(part, pair_in, 0).start()
-        to_pair(scaled.at[0], scaled.at[0], 1).wait_recv()
+        to_pair(scaled, scaled, 1).wait_recv()
         to_pair(part, pair_in, 0).wait_send()
 
     @pl.when(side == 1)
@@ -197,29 +197,29 @@
             sum_copy(k).wait_recv()
         whole = ((part[...] + sum_in[0]) + (sum_in[1] + sum_in[2])) * weights
         first = whole.astype(jnp.bfloat16)
-        scaled[0, 0:every] = first
-        scaled[0, every:2 * every] = (whole - first.astype(jnp.float32)).astype(jnp.bfloat16)
+        scaled[0:every] = first
+        scaled[every:2 * every] = (whole - first.astype(jnp.float32)).astype(jnp.bfloat16)
         scaled_copy(0).start()
-        to_pair(scaled.at[0], scaled.at[0], 1).start()
+        to_pair(scaled, scaled, 1).start()
         scaled_copy(1).start()
 
     parts = ((1, 0), (1, 1), (0, 0), (0, 1))
 
-    def product(which, factor_part):
-        both = jnp.dot(scaled[which], factor_part.reshape(plane_rank, piece),
+    def product(values, factor_part):
+        return jnp.dot(values, factor_part.reshape(plane_rank, piece),
                        preferred_element_type=jnp.float32)
-        return both[:every] + both[every:]
 
     for part_index, k in parts:
         columns = span(2 * height_at(2 * part_index) + k, piece)
-        terms[part_index, k] = product(0, factor_in[:, :, columns])
+        both = product(scaled[...], factor_in[:, :, columns])
+        terms[part_index, k] = both[:every] + both[every:]
     for part_index in (1, 0):
         for k in range(plane_size):
             near_copy(part_index, k).wait_recv()
     scaled_copy(0).wait_recv()
     for part_index, k in parts:
         near_part = near_factor[part_index, :, :, k * piece:(k + 1) * piece]
-        whole = terms[part_index, k] + product(1, near_part)
+        whole = terms[part_index, k] + product(near_scaled[...], near_part)
         if part_index:
             terms_out[k] = whole.astype(jnp.bfloat16)
             terms_copy(k).start()
@@ -323,7 +323,8 @@
     def turn(i, k):
         z = height(i)
         side_copy(z, k, k, True).wait_recv()
-        for_cores(at_corner(i, k), lambda: None, lambda: corner_copy(z, 1 - k).start())
+        if i != 1:
+            for_cores(at_corner(i, k), lambda: None, lambda: corner_copy(z, 1 - k).start())
 
     def add_own(i):
         add_scores(height(i), False, False)
@@ -333,10 +334,20 @@
         side_copy(z, 1 - along, along, True).wait_recv()
         add_scores(z, along == 0, along == 1)
 
+    def share_copy(k):
+        ref = piece_of(block(pz, True, True), k)
+        return to_chip(ref, ref, corner_send.at[1 - k, height(1)], corner_recv.at[1 - k, pz], chip(1, 0))
+
+    def share():
+        for k in range(2):
+            corner_copy(pz, 1 - k, True).wait_recv()
+            share_copy(k).start()
+
     def add_corner(i):
         z = height(i)
-        for along in range(2):
-            corner_copy(z, along, True).wait_recv()
+        if i > 0:
+            for along in range(2):
+                corner_copy(z, along, True).wait_recv()
         add_scores(z, True, True)
 
     arrive(0, 0)
@@ -364,19 +375,20 @@
     turn(1, 1)
     add_side(1, 0)
     add_side(1, 1)
+    share()
     arrive(3, 1)
     spread(3, 1)
     turn(2, 0)
     add_own(3)
-    add_corner(0)
     turn(2, 1)
     add_side(2, 0)
     add_side(2, 1)
+    add_corner(0)
     turn(3, 0)
-    add_corner(1)
     turn(3, 1)
     add_side(3, 0)
     add_side(3, 1)
+    add_corner(1)
     add_corner(2)
     add_corner(3)
     other_rows = pl.ds(pl.multiple_of((1 - side) * half, half), half)
@@ -400,7 +412,7 @@
     def _():
         for k in range(1, plane_size):
             sum_copy(k).wait_send()
-        to_pair(scaled.at[0], scaled.at[0], 1).wait_send()
+        to_pair(scaled, scaled, 1).wait_send()
         for core in range(2):
             scaled_copy(core).wait_send()
 
@@ -445,7 +457,8 @@
             pltpu.VMEM((every, plane_rank), f32),
             pltpu.VMEM((every, plane_rank), f32),
             pltpu.VMEM((plane_size - 1, every, plane_rank), f32),
-            pltpu.VMEM((2, 2 * every, plane_rank), bf16),
+            pltpu.VMEM((2 * every, plane_rank), bf16),
+            pltpu.VMEM((every, plane_rank), bf16),
             pltpu.VMEM((2, 2, every, width // 2), f32),
             pltpu.VMEM((2, every, width // 2), bf16),
             pltpu.VMEM((2, every, width // 2), bf16),

time: 63.5 us -> 61.3 us (0.965)
  Pallas kernels: 61.1 us -> 59.1 us
    pallas_call x1, Pallas kernels: 61.1 us -> 59.1 us  [fused(): pl.pallas_call(functools.partial(fused_kernel, nb), out_shape=jax.ShapeDt...]
where the time goes in v3:
time: 61.3 us; the launch traced here: 61.1 us
  Pallas kernels  59.1 us (96%)
  local copies, waits for them, and re-layouts  1.34 us (2%)
  between operations  0.67 us (1%)
    pallas_call x1, Pallas kernels, fused(): pl.pallas_call(functools.partial(fused_kernel, nb), out_shape=jax.ShapeDt...  59.1 us
    unnamed x3, local copies, waits for them, and re-layouts  1.34 us

profile of v3, /device:TPU:0, one launch (start us, length us, event | category | flops | bytes accessed | tf_op | source)
XLA Modules:
  0.0 61.1 jit_solution(12525193804283123396)
XLA Ops:
  0.7 0.0 copy-start
  0.7 0.7 %copy-done = f32[1024]{0:T(1024)S(1)} copy-done((f32[1024]{0:T(1024)S(1)}, f32[1024]{0:T(1024)}, u32[]{:S(2)}) %copy-start) | copy-done | bytes 4120
  1.3 59.1 %shard_map.55 = bf16[64,1024]{1,0:T(8,128)(2,1)S(1)} custom-call(bf16[8,8192]{1,0:T(8,128)(2,1)} %queries.1, bf16[64,8192]{1,0:T(8,128)(2,1)} %bitcast.3, f32[1,1024]{1,0:T(1,128)S(1)} %bitcast.2, f32[1]{0:T(128)S(6)} %copy.7.damping, bf16[1024,8192]{1,0:T(8,128)(2,1)} %train_rows.1), custom_call_target="tpu_custom_call" | custom-call | tf_op jit(solution)/shard_map/pallas_call | solution.py:445
  60.4 0.7 %copy.8 = bf16[64,1024]{1,0:T(8,128)(2,1)} copy(bf16[64,1024]{1,0:T(8,128)(2,1)S(1)} %shard_map.55) | data formatting | bytes 262144
Async XLA Ops:
  0.7 0.7 %copy-start = (f32[1024]{0:T(1024)S(1)}, f32[1024]{0:T(1024)}, u32[]{:S(2)}) copy-start(f32[1024]{0:T(1024)} %param.7) | copy-start | bytes 12292

commit v4 on v3

--- a/solution.py
+++ b/solution.py
@@ -13,10 +13,10 @@
 
 def fused_kernel(
     nb, queries, factor_t, eigenvalues, damping, train_rows, out,
-    query_out, factor_out, query_in, factor_in, near_factor, train_in, part, pair_in, sum_in, scaled, near_scaled,
-    terms, terms_out, terms_in, pre, total, total_in,
+    query_out, factor_out, query_in, factor_in, near_factor, train_in, part, pair_in, sum_out, sum_in, scaled, near_scaled,
+    terms, terms_out, terms_in, beside_out, beside_in, pre, total, total_in,
     train_sem, load_sem, query_send, query_recv, factor_send, factor_recv, near_send, near_recv,
-    rows_send, rows_recv, sum_send, sum_recv, scaled_send, scaled_recv, terms_send, terms_recv,
+    rows_send, rows_recv, sum_send, sum_recv, scaled_send, scaled_recv, terms_send, terms_recv, beside_send, beside_recv,
     line_send, line_recv, far_send, side_send, side_recv, corner_send, corner_recv, pair_send, pair_recv,
 ):
     me = lax.axis_index("blk")
@@ -83,7 +83,7 @@
                        rows_send.at[d - 1, k], rows_recv.at[d - 1, k], chip(d, 0))
 
     def sum_copy(k):
-        return to_chip(part, sum_in.at[k - 1], sum_send.at[k - 1], sum_recv.at[k - 1], chip(0, k))
+        return to_chip(sum_out, sum_in.at[k - 1], sum_send.at[k - 1], sum_recv.at[k - 1], chip(0, k))
 
     def near_copy(part_index, k):
         columns = span(height_at(3 if part_index else 1), width)
@@ -95,6 +95,9 @@
             src_ref=scaled.at[0:every], dst_ref=near_scaled,
             send_sem=scaled_send.at[core], recv_sem=scaled_recv.at[0],
             device_id={"blk": chip(1, 0), "col": core}, device_id_type=MESH)
+
+    def beside_copy(k):
+        return to_chip(beside_out.at[k], beside_in.at[k], beside_send.at[k], beside_recv.at[k], chip(1, 0))
 
     def terms_copy(k):
         return to_chip(terms_out.at[k], terms_in.at[k], terms_send.at[k], terms_recv.at[k], chip(2, 0))
@@ -152,7 +155,7 @@
     for d in (2, 3, 1):
         rows_copy(d, 0, me).start()
     load_factor(0).wait()
-    for part_index in (1, 0):
+    for part_index in (1,):
         near_copy(part_index, 0).start()
 
     def start_train(k, carry):
@@ -164,15 +167,14 @@
         query_copy(k, chip(0, k)).wait_recv()
         for d in (2, 3, 1):
             rows_copy(d, k, chip(0, k)).start()
-    for k in (1, 2, 3):
-        factor_copy(k, spot(k)).wait_recv()
-        for part_index in (1, 0):
-            near_copy(part_index, k).start()
     for d in range(1, line):
         for k in range(plane_size):
             rows_copy(d, k, chip(d, k)).wait_recv()
-
     query_wide = query_in[...].astype(jnp.float32).reshape(every, wide).astype(jnp.bfloat16)
+    for k in (1, 2, 3):
+        factor_copy(k, spot(k)).wait_recv()
+        for part_index in (1,):
+            near_copy(part_index, k).start()
     partial_value = lax.dot_general(
         query_wide, factor_in[...].reshape(plane_rank, wide),
         CONTRACT_LAST, preferred_element_type=jnp.float32)
@@ -191,11 +193,13 @@
     def _():
         to_pair(part, pair_in, 0).wait_recv()
         part[...] = part[...] + pair_in[...]
+        sum_out[...] = part[...].astype(jnp.bfloat16)
         for k in (3, 1, 2):
             sum_copy(k).start()
         for k in (1, 2, 3):
             sum_copy(k).wait_recv()
-        whole = ((part[...] + sum_in[0]) + (sum_in[1] + sum_in[2])) * weights
+        arrived = [sum_in[k].astype(jnp.float32) for k in range(3)]
+        whole = ((part[...] + arrived[0]) + (arrived[1] + arrived[2])) * weights
         first = whole.astype(jnp.bfloat16)
         scaled[0:every] = first
         scaled[every:2 * every] = (whole - first.astype(jnp.float32)).astype(jnp.bfloat16)
@@ -203,33 +207,34 @@
         to_pair(scaled, scaled, 1).start()
         scaled_copy(1).start()
 
-    parts = ((1, 0), (1, 1), (0, 0), (0, 1))
-
     def product(values, factor_part):
         return jnp.dot(values, factor_part.reshape(plane_rank, piece),
                        preferred_element_type=jnp.float32)
 
-    for part_index, k in parts:
-        columns = span(2 * height_at(2 * part_index) + k, piece)
-        both = product(scaled[...], factor_in[:, :, columns])
-        terms[part_index, k] = both[:every] + both[every:]
-    for part_index in (1, 0):
-        for k in range(plane_size):
-            near_copy(part_index, k).wait_recv()
+    def plane_terms(d, k):
+        both = product(scaled[...], factor_in[:, :, span(2 * height_at(d) + k, piece)])
+        return both[:every] + both[every:]
+
+    for k in range(2):
+        beside_out[k] = plane_terms(1, k).astype(jnp.bfloat16)
+        beside_copy(k).start()
+    for k in range(2):
+        terms[1, k] = plane_terms(2, k)
+    for k in range(plane_size):
+        near_copy(1, k).wait_recv()
     scaled_copy(0).wait_recv()
-    for part_index, k in parts:
-        near_part = near_factor[part_index, :, :, k * piece:(k + 1) * piece]
-        whole = terms[part_index, k] + product(near_scaled[...], near_part)
-        if part_index:
-            terms_out[k] = whole.astype(jnp.bfloat16)
-            terms_copy(k).start()
-        else:
-            terms[part_index, k] = whole
+    for k in range(2):
+        near_part = near_factor[1, :, :, k * piece:(k + 1) * piece]
+        terms_out[k] = (terms[1, k] + product(near_scaled[...], near_part)).astype(jnp.bfloat16)
+        terms_copy(k).start()
+    for k in range(2):
+        terms[0, k] = plane_terms(0, k)
     inverse = 1.0 / damping[0]
 
     def finish_own(k):
         terms_copy(k).wait_recv()
-        whole = terms[0, k] + terms_in[k].astype(jnp.float32)
+        beside_copy(k).wait_recv()
+        whole = terms[0, k] + (terms_in[k].astype(jnp.float32) + beside_in[k].astype(jnp.float32))
         start = pl.multiple_of(pz * width + k * piece, piece)
         own = query_in[:, :, pl.ds(start, piece)].astype(jnp.float32).reshape(every, piece)
         pre[me, :, k * piece:(k + 1) * piece] = ((own - whole) * inverse).astype(jnp.bfloat16)
@@ -403,10 +408,10 @@
         for k in range(plane_size):
             rows_copy(d, k, chip(0, k)).wait_send()
     for k in range(plane_size):
-        for part_index in range(2):
-            near_copy(part_index, k).wait_send()
+        near_copy(1, k).wait_send()
     for k in range(2):
         terms_copy(k).wait_send()
+        beside_copy(k).wait_send()
 
     @pl.when(side == 1)
     def _():
@@ -456,10 +461,13 @@
             pltpu.VMEM((nb, train, width), bf16),
             pltpu.VMEM((every, plane_rank), f32),
             pltpu.VMEM((every, plane_rank), f32),
-            pltpu.VMEM((plane_size - 1, every, plane_rank), f32),
+            pltpu.VMEM((every, plane_rank), bf16),
+            pltpu.VMEM((plane_size - 1, every, plane_rank), bf16),
             pltpu.VMEM((2 * every, plane_rank), bf16),
             pltpu.VMEM((every, plane_rank), bf16),
             pltpu.VMEM((2, 2, every, width // 2), f32),
+            pltpu.VMEM((2, every, width // 2), bf16),
+            pltpu.VMEM((2, every, width // 2), bf16),
             pltpu.VMEM((2, every, width // 2), bf16),
             pltpu.VMEM((2, every, width // 2), bf16),
             pltpu.VMEM((nb, every, width), bf16),
@@ -471,7 +479,7 @@
             dma((2, plane_size)), dma((2, plane_size)),
             dma((line - 1, plane_size)), dma((line - 1, plane_size)),
             dma((plane_size - 1,)), dma((plane_size - 1,)),
-            dma((2,)), dma((1,)), dma((2,)), dma((2,)),
+            dma((2,)), dma((1,)), dma((2,)), dma((2,)), dma((2,)), dma((2,)),
             dma((2, 2 * line)), dma((2 * line,)), dma((line - 1, 2)), dma((2, 2 * line)), dma((2, 2 * line)),
             dma((2, line)), dma((2, line)), dma((3,)), dma((3,)),
         ],

time: 61.3 us -> 59.3 us (0.967)
  Pallas kernels: 59.1 us -> 57.1 us
    pallas_call x1, Pallas kernels: 59.1 us -> 57.1 us  [fused(): pl.pallas_call(functools.partial(fused_kernel, nb), out_shape=jax.ShapeDt...]
where the time goes in v4:
time: 59.3 us; the launch traced here: 59.1 us
  Pallas kernels  57.1 us (96%)
  local copies, waits for them, and re-layouts  1.34 us (2%)
  between operations  0.67 us (1%)
    pallas_call x1, Pallas kernels, fused(): pl.pallas_call(functools.partial(fused_kernel, nb), out_shape=jax.ShapeDt...  57.1 us
    unnamed x3, local copies, waits for them, and re-layouts  1.34 us

profile of v4, /device:TPU:0, one launch (start us, length us, event | category | flops | bytes accessed | tf_op | source)
XLA Modules:
  0.0 59.1 jit_solution(967122723598347691)
XLA Ops:
  0.7 0.0 copy-start
  0.7 0.7 %copy-done = f32[1024]{0:T(1024)S(1)} copy-done((f32[1024]{0:T(1024)S(1)}, f32[1024]{0:T(1024)}, u32[]{:S(2)}) %copy-start) | copy-done | bytes 4120
  1.3 57.1 %shard_map.55 = bf16[64,1024]{1,0:T(8,128)(2,1)S(1)} custom-call(bf16[8,8192]{1,0:T(8,128)(2,1)} %queries.1, bf16[64,8192]{1,0:T(8,128)(2,1)} %bitcast.3, f32[1,1024]{1,0:T(1,128)S(1)} %bitcast.2, f32[1]{0:T(128)S(6)} %copy.7.damping, bf16[1024,8192]{1,0:T(8,128)(2,1)} %train_rows.1), custom_call_target="tpu_custom_call" | custom-call | tf_op jit(solution)/shard_map/pallas_call | solution.py:450
  58.4 0.7 %copy.8 = bf16[64,1024]{1,0:T(8,128)(2,1)} copy(bf16[64,1024]{1,0:T(8,128)(2,1)S(1)} %shard_map.55) | data formatting | bytes 262144
Async XLA Ops:
  0.7 0.7 %copy-start = (f32[1024]{0:T(1024)S(1)}, f32[1024]{0:T(1024)}, u32[]{:S(2)}) copy-start(f32[1024]{0:T(1024)} %param.7) | copy-start | bytes 12292
